TPU v7x, 512 devices: a whole 4x8x8 slice. The times are simulated.
512 devices in a mesh: grp: 4 (over x), dev: 128 (over z, y, core).
Axes of the slice: x: 4, y: 8, z: 8, core: 2. Of those that a mesh axis runs over, the one named last changes fastest.
Arguments:
- blocks: bfloat16 [4096, 64, 4096], P(('grp', 'dev')), may hold values from -6 to 6
- coords: int32 [3, 4096], P(None, ('grp', 'dev')), may hold values from 0 to 255, as said below
- counts: int32 [512], P(('grp', 'dev')), may hold values from 1 to 8, as said below
- row_place: int32 [256], replicated, may hold values from 0 to 255, as said below
- factor_one: bfloat16 [256, 4096], P('dev'), may hold values from -0.75 to 0.75
- factor_two: bfloat16 [256, 4096], P('dev'), may hold values from -0.75 to 0.75
- factor_three: bfloat16 [256, 4096], P('dev'), may hold values from -0.75 to 0.75
Outputs:
- new_rows: float32 [256, 4096], P('dev')
- gram: float32 [64, 64], replicated
Inputs may be any that keep to these rules, and one draw needn't show every extreme that they name: `coords`: every mode-1 id of a slot on the device with dev index d has its row-block position in [d * 2, (d + 1) * 2); on one device, the row-block positions of the mode-2 ids of its 8 slots lie in pairwise different ranges [e * 2, (e + 1) * 2), and so do those of the mode-3 ids. `counts`: some device has all 8 slots live. `row_place`: A permutation of 0 to 255.
All inputs are finite; a program needn't handle non-finite values.
Results may differ from a plain program's by a relative error of at most 0.0056.
Values may be sent and summed in bfloat16 or wider, within the bound.
A program may use at most 128 MiB of HBM per device.

v0:
```python
import jax
import jax.numpy as jnp
from jax import lax
from jax.sharding import PartitionSpec as P


def look_place(ids, row_place):
    table = jnp.arange(row_place.shape[0])
    hits = ids[:, None] == table[None, :]
    return jnp.sum(jnp.where(hits, row_place[None, :], 0), axis=1)


def body(blocks, coords, counts, row_place, factor_one, factor_two, factor_three):
    slot_count = blocks.shape[0]
    edge = blocks.shape[1]
    rank_width = factor_one.shape[1] // edge
    row_blocks = factor_one.shape[0]
    live = (jnp.arange(slot_count) < counts[0]).astype(jnp.float32)
    pos_one = look_place(coords[0], row_place)
    pos_two = look_place(coords[1], row_place)
    pos_three = look_place(coords[2], row_place)
    local_one = pos_one % row_blocks
    pieces = (
        lax.all_gather(factor_two, "dev", axis=0, tiled=True),
        lax.all_gather(factor_three, "dev", axis=0, tiled=True),
    )
    taken = pieces[0].shape[0]
    offsets = jnp.arange(taken)
    pick_two = (pos_two[:, None] == offsets[None, :]).astype(jnp.bfloat16)
    pick_three = (pos_three[:, None] == offsets[None, :]).astype(jnp.bfloat16)
    chosen_two = jnp.dot(pick_two, pieces[0], preferred_element_type=jnp.float32)
    chosen_three = jnp.dot(pick_three, pieces[1], preferred_element_type=jnp.float32)
    upper = chosen_two.astype(jnp.bfloat16).reshape(slot_count, edge, rank_width)
    lower = chosen_three.astype(jnp.bfloat16).reshape(slot_count, edge, rank_width)
    tensor_rows = blocks.reshape(slot_count, edge * edge, edge)
    first = jnp.einsum(
        "bmk,bks->bms", tensor_rows, lower, preferred_element_type=jnp.float32
    ).astype(jnp.bfloat16)
    first = first.reshape(slot_count, edge, edge, rank_width)
    contrib = jnp.einsum("bajs,bjr->bars", first, upper, preferred_element_type=jnp.float32)
    contrib = contrib.reshape(slot_count, edge, rank_width * rank_width)
    owners = jnp.arange(row_blocks)
    assign = (local_one[:, None] == owners[None, :]).astype(jnp.float32) * live[:, None]
    panels = jnp.einsum("bl,bam->lam", assign, contrib, precision=lax.Precision.HIGHEST)
    panels = panels.reshape(row_blocks * edge, rank_width * rank_width)
    old_rows = factor_one.reshape(row_blocks * edge, rank_width)
    summed = lax.psum(panels, "grp")
    panel_b = summed.astype(jnp.bfloat16)
    proj_terms = jnp.dot(panel_b.T, old_rows, preferred_element_type=jnp.float32)
    proj = lax.psum(proj_terms, "dev").astype(jnp.bfloat16)
    rows = jnp.dot(panel_b, proj, preferred_element_type=jnp.float32)
    gram_local = jnp.dot(
        rows.T, rows, precision=lax.Precision.HIGHEST, preferred_element_type=jnp.float32
    )
    gmat = lax.psum(gram_local, "dev")
    trace_value = jnp.trace(gmat)
    rows_total = row_blocks * edge * lax.axis_size("dev")
    new_rows = (rows * lax.rsqrt(trace_value / (rows_total * rank_width))).reshape(
        row_blocks, edge * rank_width
    )
    gram = gmat * (rank_width / trace_value)
    return (new_rows, gram)


def solution(mesh):
    placed = (
        P(("grp", "dev"), None, None),
        P(None, ("grp", "dev")),
        P(("grp", "dev")),
        P(),
        P("dev", None),
        P("dev", None),
        P("dev", None),
    )
    return jax.shard_map(
        body, mesh=mesh, in_specs=placed, out_specs=(P("dev", None), P()), check_vma=False
    )
```

profile of v0, /device:TPU:4, one launch (start us, length us, event | category | flops | bytes accessed | tf_op | source)
XLA Modules:
  0.0 1270.0 jit_solution(4635308471587969259)
XLA Ops:
  7.2 0.0 copy-start
  7.2 0.0 copy-start.1
  7.2 0.0 copy-start.2
  7.2 0.0 all-gather.7.cloned.1.call-start
  7.2 0.7 all-gather.7.cloned.1.call-update
  7.9 0.0 all-gather.5.cloned.1.call-start
  8.0 0.7 all-gather.5.cloned.1.call-update
  8.7 12.6 reshape.54
  21.9 0.0 copy-done
  21.9 0.1 reshape.58
  22.0 0.0 copy-done.1
  22.0 0.0 copy-done.2
  22.1 0.2 select_reduce_fusion.3
  22.3 76.6 %all-gather.7.cloned.1.call-done = bf16[128,2,4096]{2,1,0:T(2,128)(2,1)} async-done(((bf16[1,2,4096]{2,1,0:T(2,128)(2,1)}), bf16[128,2,4096]{2,1,0:T(2,128)(2,1)}) %all-gather.7.cloned.1.call-update) | async-done | bytes 2097168 | tf_op jit(solution)/shard_map/all_gather | solution.py:25
  98.9 2.7 reshape.63
  101.6 0.4 convolution_convert_fusion.1
  102.0 0.2 reshape.53
  102.2 8.4 fusion.2
  110.7 8.4 copy.40
  119.0 62.9 %all-gather.5.cloned.1.call-done = bf16[128,2,4096]{2,1,0:T(2,128)(2,1)} async-done(((bf16[1,2,4096]{2,1,0:T(2,128)(2,1)}), bf16[128,2,4096]{2,1,0:T(2,128)(2,1)}) %all-gather.5.cloned.1.call-update) | async-done | bytes 2097168 | tf_op jit(solution)/shard_map/all_gather | solution.py:24
  181.9 2.7 reshape.61
  184.7 0.4 convolution_convert_fusion.2
  185.1 0.2 reshape.52
  185.3 11.5 convolution_bitcast_fusion
  196.8 14.8 %reshape.56 = f32[8,64,4096]{2,1,0:T(8,128)} reshape(f32[8,64,64,64]{3,2,1,0:T(8,128)} %convolution_bitcast_fusion) | data formatting | bytes 16777216 | tf_op jit(solution)/shard_map/reshape | solution.py:41
  211.5 15.3 %fusion = f32[2,64,4096]{2,0,1:T(2,128)S(1)} fusion(f32[8,64,4096]{2,1,0:T(8,128)} %reshape.56, f32[8]{0:T(128)S(1)} %compare_convert_fusion, s32[8]{0:T(128)S(1)} %and_select_fusion), kind=kOutput, calls=%fused_computation.1 | convolution fusion | flops 50331680 | bytes 10485824 | tf_op jit(solution)/shard_map/bl,bam->lam/dot_general | solution.py:44
  226.8 1.2 copy.33
  228.1 42.2 %all-reduce.2 = bf16[128,4096]{1,0:T(8,128)(2,1)S(1)} all-reduce(f32[128,4096]{1,0:T(8,128)S(1)} %bitcast.38), channel_id=1, replica_groups=mesh['grp'=4,'dev'=128] {'grp'}, use_global_device_ids=true, to_apply=%region_3.4 | all-reduce | flops 524288 | bytes 3145728 | tf_op jit(solution)/shard_map/psum | solution.py:47
  270.2 0.3 fusion.21
  270.6 497.6 %all-reduce.3 = bf16[4096,64]{0,1:T(8,128)(2,1)S(1)} all-reduce(f32[4096,64]{0,1:T(8,128)S(1)} %fusion.21), channel_id=1, replica_groups=mesh['grp'=4,'dev'=128] {'dev'}, use_global_device_ids=true, to_apply=%region_4.5 | all-reduce | flops 262144 | bytes 1572864 | tf_op jit(solution)/shard_map/psum | solution.py:50
  768.2 0.5 fusion.20
  768.7 0.2 fusion.19
  768.9 490.9 %psum.23 = f32[64,64]{1,0:T(8,128)S(1)} all-reduce(f32[64,64]{1,0:T(8,128)S(1)} %fusion.19), channel_id=1, replica_groups=mesh['grp'=4,'dev'=128] {'dev'}, use_global_device_ids=true, to_apply=%region_5.6 | all-reduce | flops 4096 | bytes 32768 | tf_op jit(solution)/shard_map/psum | solution.py:55
  1259.7 0.6 select_reduce_fusion
  1261.0 0.6 broadcast_multiply_fusion
  1262.4 0.1 copy.34
  1262.4 0.7 reshape.59
  (4 shorter events, 0.0 us)
Async XLA Ops:
  7.2 14.7 %copy-start = (bf16[2,4096]{1,0:T(2,128)(2,1)S(1)}, bf16[2,4096]{1,0:T(2,128)(2,1)}, u32[]{:S(2)}) copy-start(bf16[2,4096]{1,0:T(2,128)(2,1)} %param.11) | copy-start | bytes 49156
  7.2 14.8 %copy-start.1 = (s32[3,8]{1,0:T(4,128)S(1)}, s32[3,8]{1,0:T(4,128)}, u32[]{:S(2)}) copy-start(s32[3,8]{1,0:T(4,128)} %param.8) | copy-start | bytes 292
  7.2 14.9 %copy-start.2 = (s32[256]{0:T(256)S(1)}, s32[256]{0:T(256)}, u32[]{:S(2)}) copy-start(s32[256]{0:T(256)} %param.10) | copy-start | bytes 3076
  7.2 91.7 %all-gather.7.cloned.1.call-start = ((), (), s32[]{:S(2)}) async-start(), calls=%async_computation.1 | async-start | bytes 2113536 | tf_op jit(solution)/shard_map/all_gather | solution.py:25
  7.9 174.0 %all-gather.5.cloned.1.call-start = ((), (), s32[]{:S(2)}) async-start(), calls=%async_computation | async-start | bytes 2113536 | tf_op jit(solution)/shard_map/all_gather | solution.py:24
Sparse Core Ops, SparseCore 0:
  11.1 87.6 all-gather.6
  102.0 79.9 all-gather.4
where the time goes:
time: 1270 us
  blocking collectives  1030 us (81%)
  waiting for transfers between devices  141 us (11%)
  local copies, waits for them, and re-layouts  43.7 us (3%)
  matrix products  37 us (3%)
  between operations  16.2 us (1%)
    psum x1, blocking collectives, body(): proj = lax.psum(proj_terms, 'dev').astype(jnp.bfloat16)  498 us
    psum x1, blocking collectives, body(): gmat = lax.psum(gram_local, 'dev')  491 us
    all_gather x1, waiting for transfers between devices, body(): lax.all_gather(factor_three, 'dev', axis=0, tiled=True)  76.6 us
    all_gather x1, waiting for transfers between devices, body(): lax.all_gather(factor_two, 'dev', axis=0, tiled=True)  62.9 us
    psum x1, blocking collectives, body(): summed = lax.psum(panels, 'grp')  42.2 us
  transfers between devices with their start and end apart: 2, of which 2 were waited for; matrix products, arithmetic and copies ran while one was open for 3% of the time, Pallas kernels for 0%

commit v1 on v0

--- a/solution.py
+++ b/solution.py
@@ -52,7 +52,8 @@
     gram_local = jnp.dot(
         rows.T, rows, precision=lax.Precision.HIGHEST, preferred_element_type=jnp.float32
     )
-    gmat = lax.psum(gram_local, "dev")
+    shards = lax.all_gather(gram_local, "dev")
+    gmat = jnp.sum(shards, axis=0)
     trace_value = jnp.trace(gmat)
     rows_total = row_blocks * edge * lax.axis_size("dev")
     new_rows = (rows * lax.rsqrt(trace_value / (rows_total * rank_width))).reshape(

time: 1270 us -> 863 us (0.68)
  the two profiles are of different devices: /device:TPU:4 before, /device:TPU:1 now
where the time goes in v1:
time: 863 us; the launch traced here: 862 us
  blocking collectives  536 us (62%)
  waiting for transfers between devices  225 us (26%)
  local copies, waits for them, and re-layouts  43.7 us (5%)
  matrix products  37.7 us (4%)
  between operations  15.9 us (2%)
    psum x1, blocking collectives, body(): proj = lax.psum(proj_terms, 'dev').astype(jnp.bfloat16)  494 us
    all_gather x1, waiting for transfers between devices, body(): shards = lax.all_gather(gram_local, 'dev')  82.7 us
    all_gather x1, waiting for transfers between devices, body(): lax.all_gather(factor_three, 'dev', axis=0, tiled=True)  77.8 us
    all_gather x1, waiting for transfers between devices, body(): lax.all_gather(factor_two, 'dev', axis=0, tiled=True)  62.9 us
    psum x1, blocking collectives, body(): summed = lax.psum(panels, 'grp')  42.2 us
  transfers between devices with their start and end apart: 3, of which 3 were waited for; matrix products, arithmetic and copies ran while one was open for 4% of the time, Pallas kernels for 0%

profile of v1, /device:TPU:1, one launch (start us, length us, event | category | flops | bytes accessed | tf_op | source)
XLA Modules:
  0.0 862.0 jit_solution(7118439971676732521)
XLA Ops:
  7.2 0.0 all-gather.11.cloned.1.call-start
  7.2 0.7 all-gather.11.cloned.1.call-update
  7.9 0.0 all-gather.9.cloned.1.call-start
  7.9 0.7 all-gather.9.cloned.1.call-update
  8.6 0.0 copy-start
  8.7 0.0 copy-start.1
  8.7 0.0 copy-start.2
  8.7 0.0 all-gather.7.cloned.1.call-start
  8.7 12.6 %reshape.54 = bf16[8,4096,64]{2,1,0:T(8,128)(2,1)} reshape(bf16[8,64,4096]{2,1,0:T(8,128)(2,1)} %param.7) | data formatting | bytes 8388608 | tf_op jit(solution)/shard_map/reshape | solution.py:35
  21.9 0.0 copy-done
  22.0 0.1 reshape.58
  22.1 0.0 copy-done.1
  22.1 0.0 copy-done.2
  22.1 0.2 select_reduce_fusion.3
  22.3 77.8 %all-gather.11.cloned.1.call-done = bf16[128,2,4096]{2,1,0:T(2,128)(2,1)} async-done(((bf16[1,2,4096]{2,1,0:T(2,128)(2,1)}), bf16[128,2,4096]{2,1,0:T(2,128)(2,1)}) %all-gather.11.cloned.1.call-update) | async-done | bytes 2097168 | tf_op jit(solution)/shard_map/all_gather | solution.py:25
  100.1 2.7 reshape.64
  102.8 0.4 convolution_convert_fusion.1
  103.3 0.2 reshape.53
  103.4 8.4 fusion.2
  111.9 8.4 copy.40
  120.2 62.9 %all-gather.9.cloned.1.call-done = bf16[128,2,4096]{2,1,0:T(2,128)(2,1)} async-done(((bf16[1,2,4096]{2,1,0:T(2,128)(2,1)}), bf16[128,2,4096]{2,1,0:T(2,128)(2,1)}) %all-gather.9.cloned.1.call-update) | async-done | bytes 2097168 | tf_op jit(solution)/shard_map/all_gather | solution.py:24
  183.2 2.7 reshape.62
  185.9 0.4 convolution_convert_fusion.2
  186.3 0.2 reshape.52
  186.5 11.5 %convolution_bitcast_fusion = f32[8,64,64,64]{3,2,1,0:T(8,128)} fusion(bf16[8,64,64,64]{3,2,1,0:T(8,128)(2,1)} %bitcast.38, bf16[8,64,64]{2,1,0:T(8,128)(2,1)S(1)} %reshape.52), kind=kOutput, calls=%fused_computation | convolution fusion | flops 268435456 | bytes 12648448 | tf_op jit(solution)/shard_map/bajs,bjr->bars/dot_general | solution.py:40
  198.0 14.8 %reshape.56 = f32[8,64,4096]{2,1,0:T(8,128)} reshape(f32[8,64,64,64]{3,2,1,0:T(8,128)} %convolution_bitcast_fusion) | data formatting | bytes 16777216 | tf_op jit(solution)/shard_map/reshape | solution.py:41
  212.8 15.3 %fusion = f32[2,64,4096]{2,0,1:T(2,128)S(1)} fusion(f32[8,64,4096]{2,1,0:T(8,128)} %reshape.56, f32[8]{0:T(128)S(1)} %compare_convert_fusion, s32[8]{0:T(128)S(1)} %and_select_fusion), kind=kOutput, calls=%fused_computation.1 | convolution fusion | flops 50331680 | bytes 10485824 | tf_op jit(solution)/shard_map/bl,bam->lam/dot_general | solution.py:44
  228.1 1.2 copy.33
  229.3 42.2 %all-reduce.2 = bf16[128,4096]{1,0:T(8,128)(2,1)S(1)} all-reduce(f32[128,4096]{1,0:T(8,128)S(1)} %bitcast.39), channel_id=1, replica_groups=mesh['grp'=4,'dev'=128] {'grp'}, use_global_device_ids=true, to_apply=%region_3.4 | all-reduce | flops 524288 | bytes 3145728 | tf_op jit(solution)/shard_map/psum | solution.py:47
  271.5 0.3 fusion.21
  271.9 493.7 %all-reduce.3 = bf16[4096,64]{0,1:T(8,128)(2,1)S(1)} all-reduce(f32[4096,64]{0,1:T(8,128)S(1)} %fusion.21), channel_id=1, replica_groups=mesh['grp'=4,'dev'=128] {'dev'}, use_global_device_ids=true, to_apply=%region_4.5 | all-reduce | flops 262144 | bytes 1572864 | tf_op jit(solution)/shard_map/psum | solution.py:50
  765.6 0.5 fusion.20
  766.1 0.8 fusion.19
  766.9 0.0 all-gather.7.cloned.1.call-update
  766.9 82.7 %all-gather.7.cloned.1.call-done = f32[8192,64]{1,0:T(8,128)} async-done(((f32[64,64]{1,0:T(8,128)}), f32[8192,64]{1,0:T(8,128)}) %all-gather.7.cloned.1.call-update) | async-done | bytes 2097168 | tf_op jit(solution)/shard_map/all_gather | solution.py:55
  849.6 2.5 reduce_sum.49
  852.1 0.6 select_reduce_fusion
  853.4 0.6 broadcast_multiply_fusion
  854.7 0.1 copy.34
  854.8 0.7 reshape.59
  (4 shorter events, 0.0 us)
Async XLA Ops:
  7.2 92.9 %all-gather.11.cloned.1.call-start = ((), (), s32[]{:S(2)}) async-start(), calls=%async_computation.2 | async-start | bytes 2113536 | tf_op jit(solution)/shard_map/all_gather | solution.py:25
  7.9 175.3 %all-gather.9.cloned.1.call-start = ((), (), s32[]{:S(2)}) async-start(), calls=%async_computation.1 | async-start | bytes 2113536 | tf_op jit(solution)/shard_map/all_gather | solution.py:24
  8.6 13.3 %copy-start = (bf16[2,4096]{1,0:T(2,128)(2,1)S(1)}, bf16[2,4096]{1,0:T(2,128)(2,1)}, u32[]{:S(2)}) copy-start(bf16[2,4096]{1,0:T(2,128)(2,1)} %param.11) | copy-start | bytes 49156
  8.7 13.4 %copy-start.1 = (s32[3,8]{1,0:T(4,128)S(1)}, s32[3,8]{1,0:T(4,128)}, u32[]{:S(2)}) copy-start(s32[3,8]{1,0:T(4,128)} %param.8) | copy-start | bytes 292
  8.7 13.4 %copy-start.2 = (s32[256]{0:T(256)S(1)}, s32[256]{0:T(256)}, u32[]{:S(2)}) copy-start(s32[256]{0:T(256)} %param.10) | copy-start | bytes 3076
  8.7 840.9 %all-gather.7.cloned.1.call-start = ((), (), s32[]{:S(2)}) async-start(), calls=%async_computation | async-start | bytes 4227072 | tf_op jit(solution)/shard_map/all_gather | solution.py:55
Sparse Core Ops, SparseCore 0:
  11.1 88.9 all-gather.10
  103.2 79.9 all-gather.8
  767.0 82.5 all-gather.6
